TPU v7x, 32 devices: a whole 2x2x4 slice. The times are simulated.
32 devices in a mesh: chan: 8 (over z, x), src: 4 (over y, core).
Axes of the slice: x: 2, y: 2, z: 4, core: 2. Of those that a mesh axis runs over, the one named last changes fastest.
Arguments:
- records: bfloat16 [1024, 4096], P('chan'), may hold values from -600 to 600
- virtual_sources: int32 [64], P('src'), may hold values from 0 to 1023
- pair_group: int32 [4096, 1], P(('chan', 'src')), may hold values from 0 to 7; in each aligned block of 128 rows (0 to 127, 128 to 255, ...) at most 32 rows name the same one
- pair_receiver: int32 [4096], P(('chan', 'src')), may hold values from 0 to 127
- pair_source: int32 [4096], P(('chan', 'src')), may hold values from 0 to 15
- observed: float32 [4096, 2048], P(('chan', 'src')), may hold values from -6 to 6
Outputs:
- adjoint_source: float32 [1024, 4096], P(('chan', 'src'))
- pair_misfit: float32 [4096], P(('chan', 'src'))
Inputs may be any that keep to these rules, and one draw needn't show every extreme that they name: `pair_group`: among the 128 pairs listed by one device at most 32 name the same channel group, and in every draw some device lists exactly 32 pairs for some group.
All inputs are finite; a program needn't handle non-finite values.
Results may differ from a plain program's by a relative error of at most 0.0021.
Values sent between devices are 32-bit elements; how exact they have to be, the bound alone decides.
No kernel may reach another device: no remote copies, remote signals or barrier semaphores. Data moves between devices by JAX's collectives and lax.ppermute only.
A program may use at most 64 MiB of HBM per device.

v0:
```python
import math
import jax
import jax.numpy as jnp
from jax import lax
from jax.sharding import PartitionSpec as P

K0 = 64


def fourier_basis(offset, length, time_len, bin_count):
    sample_times = offset + jnp.arange(length, dtype=jnp.int32)[:, None]
    band_bins = K0 + jnp.arange(bin_count, dtype=jnp.int32)[None, :]
    phase_index = band_bins * sample_times % (2 * time_len)
    angles = phase_index.astype(jnp.float32) * (math.pi / time_len)
    return jnp.concatenate([jnp.cos(angles), -jnp.sin(angles)], axis=1)


def forward(signal_rows, bin_count):
    time_len = signal_rows.shape[1]
    block_len = min(512, time_len)

    def add_block(block_index, running):
        offset = block_index * block_len
        segment = lax.dynamic_slice_in_dim(signal_rows, offset, block_len, 1)
        fourier_table = fourier_basis(offset, block_len, time_len, bin_count).astype(jnp.bfloat16)
        return running + jnp.dot(segment, fourier_table, preferred_element_type=jnp.float32)

    return lax.fori_loop(
        0,
        time_len // block_len,
        add_block,
        jnp.zeros((signal_rows.shape[0], 2 * bin_count), jnp.float32),
    )


def inverse(spectral, time_len):
    bin_count = spectral.shape[1] // 2
    block_len = min(512, time_len)

    def fill_block(block_index, output):
        offset = block_index * block_len
        fourier_table = fourier_basis(offset, block_len, time_len, bin_count)
        values = lax.dot_general(
            spectral,
            fourier_table,
            (((1,), (1,)), ((), ())),
            precision=lax.Precision.HIGHEST,
            preferred_element_type=jnp.float32,
        ) * (1.0 / math.sqrt(bin_count))
        return lax.dynamic_update_slice_in_dim(output, values, offset, 1)

    return lax.fori_loop(
        0, time_len // block_len, fill_block, jnp.zeros((spectral.shape[0], time_len), jnp.float32)
    )


def whiten(spectra):
    bin_count = spectra.shape[1] // 2
    band_power = jnp.sum(spectra * spectra, axis=1, keepdims=True) / bin_count
    return spectra / jnp.sqrt(band_power + 1e-06)


def band_taper(bin_count):
    band_bins = jnp.arange(bin_count, dtype=jnp.int32).astype(jnp.float32)
    return 0.5 - 0.5 * jnp.cos((band_bins + 0.5) * (2.0 * math.pi / bin_count))


def pair_terms(source_rows, receiver_rows, observed_rows):
    bin_count = observed_rows.shape[-1] // 2
    weights = band_taper(bin_count)
    source_real = source_rows[..., :bin_count]
    source_imag = source_rows[..., bin_count:]
    receiver_real = receiver_rows[..., :bin_count]
    receiver_imag = receiver_rows[..., bin_count:]
    corr_real = source_real * receiver_real + source_imag * receiver_imag
    corr_imag = source_real * receiver_imag - source_imag * receiver_real
    diff_real = corr_real - observed_rows[..., :bin_count]
    diff_imag = corr_imag - observed_rows[..., bin_count:]
    misfit = jnp.sum(weights * (diff_real * diff_real + diff_imag * diff_imag), axis=-1) / (
        2 * bin_count
    )
    resid_real = weights * diff_real
    resid_imag = weights * diff_imag
    term_real = resid_real * source_real - resid_imag * source_imag
    term_imag = resid_real * source_imag + resid_imag * source_real
    return (misfit, jnp.concatenate([term_real, term_imag], axis=-1))


def per_device(records, virtual_sources, pair_group, pair_receiver, pair_source, observed):
    row_count, time_len = records.shape
    pair_count = observed.shape[0]
    bin_count = observed.shape[1] // 2
    groups = lax.axis_size("chan")
    capacity = 2 * pair_count // groups
    slot_total = groups * capacity
    chan_index = lax.axis_index("chan")
    local_rows = virtual_sources - chan_index * row_count
    inside = (local_rows >= 0) & (local_rows < row_count)
    safe_rows = jnp.clip(local_rows, 0, row_count - 1)
    whitened = whiten(forward(records, bin_count))
    picked = jnp.where(inside[:, None], jnp.take(whitened, safe_rows, axis=0), 0.0)
    sources = lax.psum(picked, "chan")
    destination = pair_group[:, 0]
    group_hits = (destination[:, None] == jnp.arange(groups, dtype=jnp.int32)[None, :]).astype(
        jnp.int32
    )
    slot_ranks = jnp.sum((jnp.cumsum(group_hits, axis=0) - 1) * group_hits, axis=1)
    slot_index = destination * capacity + slot_ranks
    send_receiver = (
        jnp.full((slot_total,), -1, jnp.int32)
        .at[slot_index]
        .set(pair_receiver)
        .reshape(groups, capacity)
    )
    send_source = (
        jnp.zeros((slot_total,), jnp.int32)
        .at[slot_index]
        .set(pair_source)
        .reshape(groups, capacity)
    )
    send_labels = jnp.stack([send_receiver, send_source], axis=-1)
    send_observed = (
        jnp.zeros((slot_total, 2 * bin_count), jnp.float32)
        .at[slot_index]
        .set(observed)
        .reshape(groups, capacity, 2 * bin_count)
    )
    observed_slots = lax.all_to_all(send_observed, "chan", split_axis=0, concat_axis=0, tiled=True)
    label_slots = lax.all_to_all(send_labels, "chan", split_axis=0, concat_axis=0, tiled=True)
    receiver_slots = label_slots[..., 0]
    source_slots = label_slots[..., 1]
    occupied = receiver_slots >= 0
    receiver_rows = jnp.take(whitened, jnp.clip(receiver_slots, 0, row_count - 1), axis=0)
    source_rows = jnp.take(sources, jnp.clip(source_slots, 0, sources.shape[0] - 1), axis=0)
    misfit, adjoint_term = pair_terms(source_rows, receiver_rows, observed_slots)
    adjoint_term = jnp.where(occupied[..., None], adjoint_term, 0.0)
    returned = lax.all_to_all(misfit, "chan", split_axis=0, concat_axis=0, tiled=True)
    arrived_terms, receivers, returned = (adjoint_term, receiver_slots, returned)
    pair_misfit = returned.reshape(slot_total)[slot_index]
    flat_terms = arrived_terms.reshape(slot_total, 2 * bin_count)
    flat_receivers = receivers.reshape(slot_total)
    selector = (jnp.arange(row_count, dtype=jnp.int32)[:, None] == flat_receivers[None, :]).astype(
        jnp.float32
    )
    adjoint_spectra = jnp.dot(
        selector, flat_terms, precision=lax.Precision.HIGHEST, preferred_element_type=jnp.float32
    )
    adjoint_source = lax.psum_scatter(
        inverse(adjoint_spectra, time_len), "src", scatter_dimension=0, tiled=True
    )
    return (adjoint_source, pair_misfit)


def solution(mesh):
    return jax.shard_map(
        per_device,
        mesh=mesh,
        in_specs=(
            P("chan", None),
            P("src"),
            P(("chan", "src"), None),
            P(("chan", "src")),
            P(("chan", "src")),
            P(("chan", "src"), None),
        ),
        out_specs=(P(("chan", "src"), None), P(("chan", "src"))),
        check_vma=False,
    )
```

profile of v0, /device:TPU:0, one launch (start us, length us, event | category | flops | bytes accessed | tf_op | source)
XLA Modules:
  0.0 358.6 jit_solution(7600043194722808114)
XLA Ops:
  12.6 7.3 %all-to-all-start = ((s32[8,32,2]{1,2,0:T(2,128)}), s32[8,32,2]{1,2,0:T(2,128)S(1)}, u32[]{:S(2)}, u32[]{:S(2)}) async-start(s32[8,32,2]{1,2,0:T(2,128)} %pad_add_fusion), calls=%async_computation | async-start | bytes 16384 | tf_op jit(solution)/shard_map/all_to_all | solution.py:129
  19.9 84.7 %while.32 = (s32[]{:T(128)}, f32[128,2048]{1,0:T(8,128)S(1)}, bf16[128,4096]{1,0:T(8,128)(2,1)}, s32[]{:T(128)}, s32[]{:T(128)}, /*index=5*/s32[]{:T(128)}, s32[]{:T(128)}) while((s32[]{:T(128)}, f32[128,2048]{1,0:T(8,128)S(1)}, bf16[128,4096]{1,0:T(8,128)(2,1)}, s32[]{:T(128)}, s32[]{:T(128)}, /*index=5*/s32[]{:T(128)}, ...), condition=%wide.region_5.6_spmd.clone, body=%wide.region_4.5_spmd.clone.sunk | while | flops 282068480 | bytes 6434957 | solution.py:28
  19.9 9.0 %cosine_convert_fusion.2 = (bf16[512,1024]{1,0:T(8,128)(2,1)S(1)}, bf16[512,1024]{1,0:T(8,128)(2,1)S(1)}) fusion(s32[512]{0:T(512)S(1)} %iota_add_fusion.10, s32[1024]{0:T(1024)S(1)} %iota_add_fusion.11), kind=kLoop, calls=%fused_computation.40.clone.1 | loop fusion | flops 8912896 | bytes 2103296 | tf_op jit(solution)/shard_map/convert
  30.5 9.0 %cosine_convert_fusion.2 = (bf16[512,1024]{1,0:T(8,128)(2,1)S(1)}, bf16[512,1024]{1,0:T(8,128)(2,1)S(1)}) fusion(s32[512]{0:T(512)S(1)} %iota_add_fusion.10, s32[1024]{0:T(1024)S(1)} %iota_add_fusion.11), kind=kLoop, calls=%fused_computation.40.clone.1 | loop fusion | flops 8912896 | bytes 2103296 | tf_op jit(solution)/shard_map/convert
  41.1 9.0 %cosine_convert_fusion.2 = (bf16[512,1024]{1,0:T(8,128)(2,1)S(1)}, bf16[512,1024]{1,0:T(8,128)(2,1)S(1)}) fusion(s32[512]{0:T(512)S(1)} %iota_add_fusion.10, s32[1024]{0:T(1024)S(1)} %iota_add_fusion.11), kind=kLoop, calls=%fused_computation.40.clone.1 | loop fusion | flops 8912896 | bytes 2103296 | tf_op jit(solution)/shard_map/convert
  51.7 9.0 %cosine_convert_fusion.2 = (bf16[512,1024]{1,0:T(8,128)(2,1)S(1)}, bf16[512,1024]{1,0:T(8,128)(2,1)S(1)}) fusion(s32[512]{0:T(512)S(1)} %iota_add_fusion.10, s32[1024]{0:T(1024)S(1)} %iota_add_fusion.11), kind=kLoop, calls=%fused_computation.40.clone.1 | loop fusion | flops 8912896 | bytes 2103296 | tf_op jit(solution)/shard_map/convert
  62.2 9.0 %cosine_convert_fusion.2 = (bf16[512,1024]{1,0:T(8,128)(2,1)S(1)}, bf16[512,1024]{1,0:T(8,128)(2,1)S(1)}) fusion(s32[512]{0:T(512)S(1)} %iota_add_fusion.10, s32[1024]{0:T(1024)S(1)} %iota_add_fusion.11), kind=kLoop, calls=%fused_computation.40.clone.1 | loop fusion | flops 8912896 | bytes 2103296 | tf_op jit(solution)/shard_map/convert
  72.8 9.0 %cosine_convert_fusion.2 = (bf16[512,1024]{1,0:T(8,128)(2,1)S(1)}, bf16[512,1024]{1,0:T(8,128)(2,1)S(1)}) fusion(s32[512]{0:T(512)S(1)} %iota_add_fusion.10, s32[1024]{0:T(1024)S(1)} %iota_add_fusion.11), kind=kLoop, calls=%fused_computation.40.clone.1 | loop fusion | flops 8912896 | bytes 2103296 | tf_op jit(solution)/shard_map/convert
  83.4 9.0 %cosine_convert_fusion.2 = (bf16[512,1024]{1,0:T(8,128)(2,1)S(1)}, bf16[512,1024]{1,0:T(8,128)(2,1)S(1)}) fusion(s32[512]{0:T(512)S(1)} %iota_add_fusion.10, s32[1024]{0:T(1024)S(1)} %iota_add_fusion.11), kind=kLoop, calls=%fused_computation.40.clone.1 | loop fusion | flops 8912896 | bytes 2103296 | tf_op jit(solution)/shard_map/convert
  94.0 9.0 %cosine_convert_fusion.2 = (bf16[512,1024]{1,0:T(8,128)(2,1)S(1)}, bf16[512,1024]{1,0:T(8,128)(2,1)S(1)}) fusion(s32[512]{0:T(512)S(1)} %iota_add_fusion.10, s32[1024]{0:T(1024)S(1)} %iota_add_fusion.11), kind=kLoop, calls=%fused_computation.40.clone.1 | loop fusion | flops 8912896 | bytes 2103296 | tf_op jit(solution)/shard_map/convert
  107.9 6.1 %all-to-all-start.1 = ((f32[8,32,2048]{2,1,0:T(8,128)}), f32[8,32,2048]{2,1,0:T(8,128)}, u32[]{:S(2)}, u32[]{:S(2)}) async-start(f32[8,32,2048]{2,1,0:T(8,128)} %bitcast.8), calls=%async_computation.1 | async-start | bytes 4194304 | tf_op jit(solution)/shard_map/all_to_all | solution.py:128
  119.0 87.0 %all-reduce.2.cloned.1.call-done = f32[16,2048]{1,0:T(8,128)} async-done(((f32[16,2048]{1,0:T(8,128)}), f32[16,2048]{1,0:T(8,128)}) %all-reduce.2.cloned.1.call-update) | async-done | bytes 131088 | tf_op jit(solution)/shard_map/psum | solution.py:102
  206.0 4.6 %gather_fusion.1 = f32[256,2048]{1,0:T(8,128)} fusion(f32[16,2048]{1,0:T(8,128)} %all-reduce.2.cloned.1.call-done, s32[1024]{0:T(1024)S(1)} %pad_clamp_fusion.2), kind=kCustom, calls=%fused_computation.1 | custom fusion | bytes 4195328 | tf_op jit(solution)/shard_map/jit(_take)/gather | solution.py:134
  210.5 3.9 %broadcast_select_fusion = (f32[8,32,2048]{2,1,0:T(8,128)}, f32[8,32,2048]{2,1,0:T(8,128)S(1)}) fusion(f32[8,32,2048]{2,1,0:T(8,128)} %bitcast.34, pred[8,32]{1,0:T(8,128)(4,1)S(1)} %get-tuple-element.220, f32[8,32,2048]{2,1,0:T(8,128)} %bitcast.35, pred[8,32]{1,0:T(8,128)(4,1)S(1)} %and_bitcast_fusion.1), kind=kLoop, calls=%fused_computation.58 | loop fusion | flops 1048576 | bytes 8389120 | tf_op jit(solution)/shard_map/jit(_take)/select_n | solution.py:133
  220.2 101.1 %while.31 = (s32[]{:T(128)}, f32[128,4096]{1,0:T(8,128)}, f32[128,2048]{1,0:T(8,128)S(1)}, s32[]{:T(128)}, s32[]{:T(128)}, /*index=5*/s32[]{:T(128)}, s32[]{:T(128)}) while((s32[]{:T(128)}, f32[128,4096]{1,0:T(8,128)}, f32[128,2048]{1,0:T(8,128)S(1)}, s32[]{:T(128)}, s32[]{:T(128)}, /*index=5*/s32[]{:T(128)}, s32[]{:T(128)}) %tuple.92), condition=%wide.region_10.11_spmd, body=%wide.region_9.10_spmd.sunk | while | flops 1619592704 | bytes 10760323 | solution.py:52
  220.2 8.3 %fusion.50 = (f32[512,1024]{1,0:T(8,128)S(1)}, f32[512,1024]{1,0:T(8,128)S(1)}) fusion(s32[512]{0:T(512)S(1)} %iota_add_fusion.8, s32[1024]{0:T(1024)S(1)} %iota_add_fusion.9), kind=kLoop, calls=%fused_computation.22.clone.1 | loop fusion | flops 7864320 | bytes 4200448 | tf_op jit(solution)/shard_map/while/body/eval_jaxpr/cos | solution.py:15
  228.5 3.4 fusion.51
  232.9 8.3 %fusion.50 = (f32[512,1024]{1,0:T(8,128)S(1)}, f32[512,1024]{1,0:T(8,128)S(1)}) fusion(s32[512]{0:T(512)S(1)} %iota_add_fusion.8, s32[1024]{0:T(1024)S(1)} %iota_add_fusion.9), kind=kLoop, calls=%fused_computation.22.clone.1 | loop fusion | flops 7864320 | bytes 4200448 | tf_op jit(solution)/shard_map/while/body/eval_jaxpr/cos | solution.py:15
  241.2 3.4 fusion.51
  245.5 8.3 %fusion.50 = (f32[512,1024]{1,0:T(8,128)S(1)}, f32[512,1024]{1,0:T(8,128)S(1)}) fusion(s32[512]{0:T(512)S(1)} %iota_add_fusion.8, s32[1024]{0:T(1024)S(1)} %iota_add_fusion.9), kind=kLoop, calls=%fused_computation.22.clone.1 | loop fusion | flops 7864320 | bytes 4200448 | tf_op jit(solution)/shard_map/while/body/eval_jaxpr/cos | solution.py:15
  253.8 3.4 fusion.51
  258.2 8.3 %fusion.50 = (f32[512,1024]{1,0:T(8,128)S(1)}, f32[512,1024]{1,0:T(8,128)S(1)}) fusion(s32[512]{0:T(512)S(1)} %iota_add_fusion.8, s32[1024]{0:T(1024)S(1)} %iota_add_fusion.9), kind=kLoop, calls=%fused_computation.22.clone.1 | loop fusion | flops 7864320 | bytes 4200448 | tf_op jit(solution)/shard_map/while/body/eval_jaxpr/cos | solution.py:15
  266.5 3.4 fusion.51
  270.8 8.3 %fusion.50 = (f32[512,1024]{1,0:T(8,128)S(1)}, f32[512,1024]{1,0:T(8,128)S(1)}) fusion(s32[512]{0:T(512)S(1)} %iota_add_fusion.8, s32[1024]{0:T(1024)S(1)} %iota_add_fusion.9), kind=kLoop, calls=%fused_computation.22.clone.1 | loop fusion | flops 7864320 | bytes 4200448 | tf_op jit(solution)/shard_map/while/body/eval_jaxpr/cos | solution.py:15
  279.1 3.4 fusion.51
  283.4 8.3 %fusion.50 = (f32[512,1024]{1,0:T(8,128)S(1)}, f32[512,1024]{1,0:T(8,128)S(1)}) fusion(s32[512]{0:T(512)S(1)} %iota_add_fusion.8, s32[1024]{0:T(1024)S(1)} %iota_add_fusion.9), kind=kLoop, calls=%fused_computation.22.clone.1 | loop fusion | flops 7864320 | bytes 4200448 | tf_op jit(solution)/shard_map/while/body/eval_jaxpr/cos | solution.py:15
  296.1 8.3 %fusion.50 = (f32[512,1024]{1,0:T(8,128)S(1)}, f32[512,1024]{1,0:T(8,128)S(1)}) fusion(s32[512]{0:T(512)S(1)} %iota_add_fusion.8, s32[1024]{0:T(1024)S(1)} %iota_add_fusion.9), kind=kLoop, calls=%fused_computation.22.clone.1 | loop fusion | flops 7864320 | bytes 4200448 | tf_op jit(solution)/shard_map/while/body/eval_jaxpr/cos | solution.py:15
  308.7 8.3 %fusion.50 = (f32[512,1024]{1,0:T(8,128)S(1)}, f32[512,1024]{1,0:T(8,128)S(1)}) fusion(s32[512]{0:T(512)S(1)} %iota_add_fusion.8, s32[1024]{0:T(1024)S(1)} %iota_add_fusion.9), kind=kLoop, calls=%fused_computation.22.clone.1 | loop fusion | flops 7864320 | bytes 4200448 | tf_op jit(solution)/shard_map/while/body/eval_jaxpr/cos | solution.py:15
  317.0 3.4 fusion.51
  321.9 3.7 %all-to-all-start.2 = ((f32[8,1,32]{2,1,0:T(1,128)}), f32[8,1,32]{2,1,0:T(1,128)S(1)}, u32[]{:S(2)}, u32[]{:S(2)}) async-start(f32[8,1,32]{2,1,0:T(1,128)} %bitcast.11), calls=%async_computation.3 | async-start | bytes 8192 | tf_op jit(solution)/shard_map/all_to_all | solution.py:137
  325.7 6.5 %all-to-all-done.2 = f32[8,1,32]{2,1,0:T(1,128)S(1)} async-done(((f32[8,1,32]{2,1,0:T(1,128)}), f32[8,1,32]{2,1,0:T(1,128)S(1)}, u32[]{:S(2)}, u32[]{:S(2)}) %all-to-all-start.2) | async-done | bytes 1056 | tf_op jit(solution)/shard_map/all_to_all | solution.py:137
  335.2 16.6 %reduce-scatter.2.cloned.1.call-done = f32[32,4096]{1,0:T(8,128)} async-done(((f32[128,4096]{1,0:T(8,128)}), f32[32,4096]{1,0:T(8,128)}) %reduce-scatter.2.cloned.1.call-update) | async-done | bytes 524304 | tf_op jit(solution)/shard_map/reduce_scatter | solution.py:148
  (107 shorter events, 49.0 us)
Async XLA Ops:
  12.6 95.3 %all-to-all-start = ((s32[8,32,2]{1,2,0:T(2,128)}), s32[8,32,2]{1,2,0:T(2,128)S(1)}, u32[]{:S(2)}, u32[]{:S(2)}) async-start(s32[8,32,2]{1,2,0:T(2,128)} %pad_add_fusion), calls=%async_computation | async-start | bytes 16384 | tf_op jit(solution)/shard_map/all_to_all | solution.py:129
  107.9 6.2 %copy-start = (s32[16]{0:T(128)S(1)}, s32[16]{0:T(128)}, u32[]{:S(2)}) copy-start(s32[16]{0:T(128)} %param.11) | copy-start | bytes 196
  107.9 106.6 %all-to-all-start.1 = ((f32[8,32,2048]{2,1,0:T(8,128)}), f32[8,32,2048]{2,1,0:T(8,128)}, u32[]{:S(2)}, u32[]{:S(2)}) async-start(f32[8,32,2048]{2,1,0:T(8,128)} %bitcast.8), calls=%async_computation.1 | async-start | bytes 4194304 | tf_op jit(solution)/shard_map/all_to_all | solution.py:128
  114.0 92.0 %all-reduce.2.cloned.1.call-start = ((), (), s32[]{:S(2)}) async-start(), calls=%async_computation.4 | async-start | bytes 262144 | tf_op jit(solution)/shard_map/psum | solution.py:102
  115.8 236.0 %reduce-scatter.2.cloned.1.call-start = ((), (), s32[]{:S(2)}) async-start(), calls=%async_computation.5 | async-start | bytes 2621440 | tf_op jit(solution)/shard_map/reduce_scatter | solution.py:148
  321.9 10.2 %all-to-all-start.2 = ((f32[8,1,32]{2,1,0:T(1,128)}), f32[8,1,32]{2,1,0:T(1,128)S(1)}, u32[]{:S(2)}, u32[]{:S(2)}) async-start(f32[8,1,32]{2,1,0:T(1,128)} %bitcast.11), calls=%async_computation.3 | async-start | bytes 8192 | tf_op jit(solution)/shard_map/all_to_all | solution.py:137
Sparse Core Ops, SparseCore 0:
  118.7 87.2 all-reduce.1
  321.5 30.2 reduce-scatter.1
where the time goes:
time: 359 us
  other arithmetic  151 us (42%)
  waiting for transfers between devices  110 us (31%)
  matrix products  40.4 us (11%)
  local copies, waits for them, and re-layouts  24.9 us (7%)
  starting transfers between devices  17.2 us (5%)
  between operations  14.2 us (4%)
    psum x1, waiting for transfers between devices, per_device(): sources = lax.psum(picked, 'chan')  87 us
    another operation x8, other arithmetic  72.2 us
    cos x8, other arithmetic, fourier_basis(): return jnp.concatenate([jnp.cos(angles), -jnp.sin(angles)], axis=1)  66.4 us
    dot_general x8, matrix products, fill_block(): lax.dot_general(spectral, fourier_table, (((1,), (1,)), ((), ())), precis...  27.4 us
    reduce_scatter x1, waiting for transfers between devices, per_device(): lax.psum_scatter(inverse(adjoint_spectra, time_len), 'src', scatter_dimen...  16.6 us
    dot_general x8, matrix products, add_block(): jnp.dot(segment, fourier_table, preferred_element_type=jnp.float32)  12 us
    all_to_all x1, starting transfers between devices, per_device(): lax.all_to_all(send_labels, 'chan', split_axis=0, concat_axis=0, tiled=True)  7.28 us
  transfers between devices with their start and end apart: 5, of which 3 were waited for; matrix products, arithmetic and copies ran while one was open for 29% of the time, Pallas kernels for 0%

commit v1 on v0

--- a/solution.py
+++ b/solution.py
@@ -1,3 +1,4 @@
+import functools
 import math
 import jax
 import jax.numpy as jnp
@@ -5,6 +6,20 @@
 from jax.sharding import PartitionSpec as P
 
 K0 = 64
+
+
+def order_pieces_all(own_rows, axis_key):
+    world_n = lax.axis_size(axis_key)
+    far_arr = own_rows
+    for src_i in [k for k in (1, 2, 4, 8, 16) if k < world_n]:
+        aux = lax.ppermute(
+            far_arr, axis_name=axis_key, perm=[(idx, idx ^ src_i) for idx in range(world_n)]
+        )
+        far_arr = far_arr + aux
+    return far_arr
+
+
+_answer_space = functools.partial(order_pieces_all, axis_key="chan")
 
 
 def fourier_basis(offset, length, time_len, bin_count):
@@ -99,7 +114,7 @@
     safe_rows = jnp.clip(local_rows, 0, row_count - 1)
     whitened = whiten(forward(records, bin_count))
     picked = jnp.where(inside[:, None], jnp.take(whitened, safe_rows, axis=0), 0.0)
-    sources = lax.psum(picked, "chan")
+    sources = _answer_space(picked)
     destination = pair_group[:, 0]
     group_hits = (destination[:, None] == jnp.arange(groups, dtype=jnp.int32)[None, :]).astype(
         jnp.int32

time: 359 us -> 319 us (0.89)
  waiting for transfers between devices: 110 us -> 65.4 us
  starting transfers between devices: 17.2 us -> 23.8 us
    psum x1 -> x0, waiting for transfers between devices: 87 us -> none  [per_device(): sources = lax.psum(picked, 'chan')]
    ppermute x0 -> x3, waiting for transfers between devices: none -> 42.2 us  [order_pieces_all(): lax.ppermute(far_arr, axis_name=axis_key, perm=[(idx, idx ^ src_i) for id...]
    ppermute x0 -> x3, starting transfers between devices: none -> 6.87 us  [order_pieces_all(): lax.ppermute(far_arr, axis_name=axis_key, perm=[(idx, idx ^ src_i) for id...]
  transfers between devices with their start and end apart: 5 -> 7, of which waited for: 3 -> 5; matrix products, arithmetic and copies ran while one was open for 29% -> 32% of each run, Pallas kernels for 0% -> 0%
where the time goes in v1:
time: 319 us; the launch traced here: 318 us
  other arithmetic  151 us (47%)
  waiting for transfers between devices  65.4 us (21%)
  matrix products  40.4 us (13%)
  starting transfers between devices  23.8 us (7%)
  local copies, waits for them, and re-layouts  23 us (7%)
  between operations  14.2 us (4%)
    another operation x8, other arithmetic  72.2 us
    cos x8, other arithmetic, fourier_basis(): return jnp.concatenate([jnp.cos(angles), -jnp.sin(angles)], axis=1)  66.4 us
    ppermute x3, waiting for transfers between devices, order_pieces_all(): lax.ppermute(far_arr, axis_name=axis_key, perm=[(idx, idx ^ src_i) for id...  42.2 us
    dot_general x8, matrix products, fill_block(): lax.dot_general(spectral, fourier_table, (((1,), (1,)), ((), ())), precis...  27.4 us
    reduce_scatter x1, waiting for transfers between devices, per_device(): lax.psum_scatter(inverse(adjoint_spectra, time_len), 'src', scatter_dimen...  16.6 us
    dot_general x8, matrix products, add_block(): jnp.dot(segment, fourier_table, preferred_element_type=jnp.float32)  12 us
    all_to_all x1, starting transfers between devices, per_device(): lax.all_to_all(send_labels, 'chan', split_axis=0, concat_axis=0, tiled=True)  7.28 us
    dynamic_update_slice x16, local copies, waits for them, and re-layouts, fill_block(): return lax.dynamic_update_slice_in_dim(output, values, offset, 1)  7.05 us
  transfers between devices with their start and end apart: 7, of which 5 were waited for; matrix products, arithmetic and copies ran while one was open for 32% of the time, Pallas kernels for 0%

profile of v1, /device:TPU:0, one launch (start us, length us, event | category | flops | bytes accessed | tf_op | source)
XLA Modules:
  0.0 318.1 jit_solution(5846212890814692909)
XLA Ops:
  12.6 7.3 %all-to-all-start = ((s32[8,32,2]{1,2,0:T(2,128)}), s32[8,32,2]{1,2,0:T(2,128)S(1)}, u32[]{:S(2)}, u32[]{:S(2)}) async-start(s32[8,32,2]{1,2,0:T(2,128)} %pad_add_fusion), calls=%async_computation | async-start | bytes 16384 | tf_op jit(solution)/shard_map/all_to_all | solution.py:144
  19.9 84.7 %while.32 = (s32[]{:T(128)}, f32[128,2048]{1,0:T(8,128)S(1)}, bf16[128,4096]{1,0:T(8,128)(2,1)}, s32[]{:T(128)}, s32[]{:T(128)}, /*index=5*/s32[]{:T(128)}, s32[]{:T(128)}) while((s32[]{:T(128)}, f32[128,2048]{1,0:T(8,128)S(1)}, bf16[128,4096]{1,0:T(8,128)(2,1)}, s32[]{:T(128)}, s32[]{:T(128)}, /*index=5*/s32[]{:T(128)}, ...), condition=%wide.region_5.6_spmd.clone, body=%wide.region_4.5_spmd.clone.sunk | while | flops 282068480 | bytes 6434957 | solution.py:43
  19.9 9.0 %cosine_convert_fusion.2 = (bf16[512,1024]{1,0:T(8,128)(2,1)S(1)}, bf16[512,1024]{1,0:T(8,128)(2,1)S(1)}) fusion(s32[512]{0:T(512)S(1)} %iota_add_fusion.10, s32[1024]{0:T(1024)S(1)} %iota_add_fusion.11), kind=kLoop, calls=%fused_computation.40.clone.1 | loop fusion | flops 8912896 | bytes 2103296 | tf_op jit(solution)/shard_map/convert
  30.5 9.0 %cosine_convert_fusion.2 = (bf16[512,1024]{1,0:T(8,128)(2,1)S(1)}, bf16[512,1024]{1,0:T(8,128)(2,1)S(1)}) fusion(s32[512]{0:T(512)S(1)} %iota_add_fusion.10, s32[1024]{0:T(1024)S(1)} %iota_add_fusion.11), kind=kLoop, calls=%fused_computation.40.clone.1 | loop fusion | flops 8912896 | bytes 2103296 | tf_op jit(solution)/shard_map/convert
  41.1 9.0 %cosine_convert_fusion.2 = (bf16[512,1024]{1,0:T(8,128)(2,1)S(1)}, bf16[512,1024]{1,0:T(8,128)(2,1)S(1)}) fusion(s32[512]{0:T(512)S(1)} %iota_add_fusion.10, s32[1024]{0:T(1024)S(1)} %iota_add_fusion.11), kind=kLoop, calls=%fused_computation.40.clone.1 | loop fusion | flops 8912896 | bytes 2103296 | tf_op jit(solution)/shard_map/convert
  51.7 9.0 %cosine_convert_fusion.2 = (bf16[512,1024]{1,0:T(8,128)(2,1)S(1)}, bf16[512,1024]{1,0:T(8,128)(2,1)S(1)}) fusion(s32[512]{0:T(512)S(1)} %iota_add_fusion.10, s32[1024]{0:T(1024)S(1)} %iota_add_fusion.11), kind=kLoop, calls=%fused_computation.40.clone.1 | loop fusion | flops 8912896 | bytes 2103296 | tf_op jit(solution)/shard_map/convert
  62.3 9.0 %cosine_convert_fusion.2 = (bf16[512,1024]{1,0:T(8,128)(2,1)S(1)}, bf16[512,1024]{1,0:T(8,128)(2,1)S(1)}) fusion(s32[512]{0:T(512)S(1)} %iota_add_fusion.10, s32[1024]{0:T(1024)S(1)} %iota_add_fusion.11), kind=kLoop, calls=%fused_computation.40.clone.1 | loop fusion | flops 8912896 | bytes 2103296 | tf_op jit(solution)/shard_map/convert
  72.8 9.0 %cosine_convert_fusion.2 = (bf16[512,1024]{1,0:T(8,128)(2,1)S(1)}, bf16[512,1024]{1,0:T(8,128)(2,1)S(1)}) fusion(s32[512]{0:T(512)S(1)} %iota_add_fusion.10, s32[1024]{0:T(1024)S(1)} %iota_add_fusion.11), kind=kLoop, calls=%fused_computation.40.clone.1 | loop fusion | flops 8912896 | bytes 2103296 | tf_op jit(solution)/shard_map/convert
  83.4 9.0 %cosine_convert_fusion.2 = (bf16[512,1024]{1,0:T(8,128)(2,1)S(1)}, bf16[512,1024]{1,0:T(8,128)(2,1)S(1)}) fusion(s32[512]{0:T(512)S(1)} %iota_add_fusion.10, s32[1024]{0:T(1024)S(1)} %iota_add_fusion.11), kind=kLoop, calls=%fused_computation.40.clone.1 | loop fusion | flops 8912896 | bytes 2103296 | tf_op jit(solution)/shard_map/convert
  94.0 9.0 %cosine_convert_fusion.2 = (bf16[512,1024]{1,0:T(8,128)(2,1)S(1)}, bf16[512,1024]{1,0:T(8,128)(2,1)S(1)}) fusion(s32[512]{0:T(512)S(1)} %iota_add_fusion.10, s32[1024]{0:T(1024)S(1)} %iota_add_fusion.11), kind=kLoop, calls=%fused_computation.40.clone.1 | loop fusion | flops 8912896 | bytes 2103296 | tf_op jit(solution)/shard_map/convert
  108.0 6.0 %all-to-all-start.1 = ((f32[8,32,2048]{2,1,0:T(8,128)}), f32[8,32,2048]{2,1,0:T(8,128)}, u32[]{:S(2)}, u32[]{:S(2)}) async-start(f32[8,32,2048]{2,1,0:T(8,128)} %bitcast.8), calls=%async_computation.1 | async-start | bytes 4194304 | tf_op jit(solution)/shard_map/all_to_all | solution.py:143
  117.2 17.3 %collective-permute-done = f32[16,2048]{1,0:T(8,128)S(1)} collective-permute-done((f32[16,2048]{1,0:T(8,128)S(1)}, f32[16,2048]{1,0:T(8,128)S(1)}, u32[]{:S(2)}, u32[]{:S(2)}) %collective-permute-start) | collective-permute-done | bytes 131104 | tf_op jit(solution)/shard_map/ppermute | solution.py:15
  135.2 15.5 %collective-permute-done.1 = f32[16,2048]{1,0:T(8,128)S(1)} collective-permute-done((f32[16,2048]{1,0:T(8,128)S(1)}, f32[16,2048]{1,0:T(8,128)S(1)}, u32[]{:S(2)}, u32[]{:S(2)}) %collective-permute-start.1) | collective-permute-done | bytes 131104 | tf_op jit(solution)/shard_map/ppermute | solution.py:15
  150.7 4.2 %collective-permute-start.2 = (f32[16,2048]{1,0:T(8,128)S(1)}, f32[16,2048]{1,0:T(8,128)S(1)}, u32[]{:S(2)}, u32[]{:S(2)}) collective-permute-start(f32[16,2048]{1,0:T(8,128)S(1)} %add.251), channel_id=1, source_target_pairs={{0,16},{4,20},{8,24},{12,28},{16,0},{20,4},{24,8},{28,12},{1,17},{... | collective-permute-start | bytes 393224 | tf_op jit(solution)/shard_map/ppermute | solution.py:15
  157.9 9.4 %collective-permute-done.2 = f32[16,2048]{1,0:T(8,128)S(1)} collective-permute-done((f32[16,2048]{1,0:T(8,128)S(1)}, f32[16,2048]{1,0:T(8,128)S(1)}, u32[]{:S(2)}, u32[]{:S(2)}) %collective-permute-start.2) | collective-permute-done | bytes 131104 | tf_op jit(solution)/shard_map/ppermute | solution.py:15
  170.1 3.9 %broadcast_select_fusion = (f32[8,32,2048]{2,1,0:T(8,128)}, f32[8,32,2048]{2,1,0:T(8,128)S(1)}) fusion(f32[8,32,2048]{2,1,0:T(8,128)} %bitcast.34, pred[8,32]{1,0:T(8,128)(4,1)S(1)} %get-tuple-element.220, f32[8,32,2048]{2,1,0:T(8,128)} %bitcast.35, pred[8,32]{1,0:T(8,128)(4,1)S(1)} %and_bitcast_fusion.1), kind=kLoop, calls=%fused_computation.58 | loop fusion | flops 1048576 | bytes 8389120 | tf_op jit(solution)/shard_map/jit(_take)/select_n | solution.py:148
  179.8 101.1 %while.31 = (s32[]{:T(128)}, f32[128,4096]{1,0:T(8,128)}, f32[128,2048]{1,0:T(8,128)S(1)}, s32[]{:T(128)}, s32[]{:T(128)}, /*index=5*/s32[]{:T(128)}, s32[]{:T(128)}) while((s32[]{:T(128)}, f32[128,4096]{1,0:T(8,128)}, f32[128,2048]{1,0:T(8,128)S(1)}, s32[]{:T(128)}, s32[]{:T(128)}, /*index=5*/s32[]{:T(128)}, s32[]{:T(128)}) %tuple.92), condition=%wide.region_9.10_spmd, body=%wide.region_8.9_spmd.sunk | while | flops 1619592704 | bytes 10760323 | solution.py:67
  179.8 8.3 %fusion.51 = (f32[512,1024]{1,0:T(8,128)S(1)}, f32[512,1024]{1,0:T(8,128)S(1)}) fusion(s32[512]{0:T(512)S(1)} %iota_add_fusion.8, s32[1024]{0:T(1024)S(1)} %iota_add_fusion.9), kind=kLoop, calls=%fused_computation.22.clone.1 | loop fusion | flops 7864320 | bytes 4200448 | tf_op jit(solution)/shard_map/while/body/eval_jaxpr/cos | solution.py:30
  188.1 3.4 %fusion.52 = f32[128,512]{0,1:T(8,128)S(1)} fusion(f32[128,2048]{1,0:T(8,128)S(1)} %get-tuple-element.307, f32[512,1024]{1,0:T(8,128)S(1)} %get-tuple-element.263, f32[512,1024]{1,0:T(8,128)S(1)} %get-tuple-element.264), kind=kOutput, calls=%fused_computation.21.clone.1 | convolution fusion | flops 1611726848 | bytes 5505024 | tf_op jit(solution)/shard_map/while/body/eval_jaxpr/dot_general | solution.py:58
  192.4 8.3 %fusion.51 = (f32[512,1024]{1,0:T(8,128)S(1)}, f32[512,1024]{1,0:T(8,128)S(1)}) fusion(s32[512]{0:T(512)S(1)} %iota_add_fusion.8, s32[1024]{0:T(1024)S(1)} %iota_add_fusion.9), kind=kLoop, calls=%fused_computation.22.clone.1 | loop fusion | flops 7864320 | bytes 4200448 | tf_op jit(solution)/shard_map/while/body/eval_jaxpr/cos | solution.py:30
  200.7 3.4 %fusion.52 = f32[128,512]{0,1:T(8,128)S(1)} fusion(f32[128,2048]{1,0:T(8,128)S(1)} %get-tuple-element.307, f32[512,1024]{1,0:T(8,128)S(1)} %get-tuple-element.263, f32[512,1024]{1,0:T(8,128)S(1)} %get-tuple-element.264), kind=kOutput, calls=%fused_computation.21.clone.1 | convolution fusion | flops 1611726848 | bytes 5505024 | tf_op jit(solution)/shard_map/while/body/eval_jaxpr/dot_general | solution.py:58
  205.1 8.3 %fusion.51 = (f32[512,1024]{1,0:T(8,128)S(1)}, f32[512,1024]{1,0:T(8,128)S(1)}) fusion(s32[512]{0:T(512)S(1)} %iota_add_fusion.8, s32[1024]{0:T(1024)S(1)} %iota_add_fusion.9), kind=kLoop, calls=%fused_computation.22.clone.1 | loop fusion | flops 7864320 | bytes 4200448 | tf_op jit(solution)/shard_map/while/body/eval_jaxpr/cos | solution.py:30
  213.4 3.4 %fusion.52 = f32[128,512]{0,1:T(8,128)S(1)} fusion(f32[128,2048]{1,0:T(8,128)S(1)} %get-tuple-element.307, f32[512,1024]{1,0:T(8,128)S(1)} %get-tuple-element.263, f32[512,1024]{1,0:T(8,128)S(1)} %get-tuple-element.264), kind=kOutput, calls=%fused_computation.21.clone.1 | convolution fusion | flops 1611726848 | bytes 5505024 | tf_op jit(solution)/shard_map/while/body/eval_jaxpr/dot_general | solution.py:58
  217.7 8.3 %fusion.51 = (f32[512,1024]{1,0:T(8,128)S(1)}, f32[512,1024]{1,0:T(8,128)S(1)}) fusion(s32[512]{0:T(512)S(1)} %iota_add_fusion.8, s32[1024]{0:T(1024)S(1)} %iota_add_fusion.9), kind=kLoop, calls=%fused_computation.22.clone.1 | loop fusion | flops 7864320 | bytes 4200448 | tf_op jit(solution)/shard_map/while/body/eval_jaxpr/cos | solution.py:30
  230.4 8.3 %fusion.51 = (f32[512,1024]{1,0:T(8,128)S(1)}, f32[512,1024]{1,0:T(8,128)S(1)}) fusion(s32[512]{0:T(512)S(1)} %iota_add_fusion.8, s32[1024]{0:T(1024)S(1)} %iota_add_fusion.9), kind=kLoop, calls=%fused_computation.22.clone.1 | loop fusion | flops 7864320 | bytes 4200448 | tf_op jit(solution)/shard_map/while/body/eval_jaxpr/cos | solution.py:30
  243.0 8.3 %fusion.51 = (f32[512,1024]{1,0:T(8,128)S(1)}, f32[512,1024]{1,0:T(8,128)S(1)}) fusion(s32[512]{0:T(512)S(1)} %iota_add_fusion.8, s32[1024]{0:T(1024)S(1)} %iota_add_fusion.9), kind=kLoop, calls=%fused_computation.22.clone.1 | loop fusion | flops 7864320 | bytes 4200448 | tf_op jit(solution)/shard_map/while/body/eval_jaxpr/cos | solution.py:30
  255.6 8.3 %fusion.51 = (f32[512,1024]{1,0:T(8,128)S(1)}, f32[512,1024]{1,0:T(8,128)S(1)}) fusion(s32[512]{0:T(512)S(1)} %iota_add_fusion.8, s32[1024]{0:T(1024)S(1)} %iota_add_fusion.9), kind=kLoop, calls=%fused_computation.22.clone.1 | loop fusion | flops 7864320 | bytes 4200448 | tf_op jit(solution)/shard_map/while/body/eval_jaxpr/cos | solution.py:30
  268.3 8.3 %fusion.51 = (f32[512,1024]{1,0:T(8,128)S(1)}, f32[512,1024]{1,0:T(8,128)S(1)}) fusion(s32[512]{0:T(512)S(1)} %iota_add_fusion.8, s32[1024]{0:T(1024)S(1)} %iota_add_fusion.9), kind=kLoop, calls=%fused_computation.22.clone.1 | loop fusion | flops 7864320 | bytes 4200448 | tf_op jit(solution)/shard_map/while/body/eval_jaxpr/cos | solution.py:30
  276.6 3.4 %fusion.52 = f32[128,512]{0,1:T(8,128)S(1)} fusion(f32[128,2048]{1,0:T(8,128)S(1)} %get-tuple-element.307, f32[512,1024]{1,0:T(8,128)S(1)} %get-tuple-element.263, f32[512,1024]{1,0:T(8,128)S(1)} %get-tuple-element.264), kind=kOutput, calls=%fused_computation.21.clone.1 | convolution fusion | flops 1611726848 | bytes 5505024 | tf_op jit(solution)/shard_map/while/body/eval_jaxpr/dot_general | solution.py:58
  281.5 3.6 %all-to-all-start.2 = ((f32[8,1,32]{2,1,0:T(1,128)}), f32[8,1,32]{2,1,0:T(1,128)S(1)}, u32[]{:S(2)}, u32[]{:S(2)}) async-start(f32[8,1,32]{2,1,0:T(1,128)} %bitcast.11), calls=%async_computation.3 | async-start | bytes 8192 | tf_op jit(solution)/shard_map/all_to_all | solution.py:152
  285.1 6.5 %all-to-all-done.2 = f32[8,1,32]{2,1,0:T(1,128)S(1)} async-done(((f32[8,1,32]{2,1,0:T(1,128)}), f32[8,1,32]{2,1,0:T(1,128)S(1)}, u32[]{:S(2)}, u32[]{:S(2)}) %all-to-all-start.2) | async-done | bytes 1056 | tf_op jit(solution)/shard_map/all_to_all | solution.py:152
  294.6 16.6 %reduce-scatter.2.cloned.1.call-done = f32[32,4096]{1,0:T(8,128)} async-done(((f32[128,4096]{1,0:T(8,128)}), f32[32,4096]{1,0:T(8,128)}) %reduce-scatter.2.cloned.1.call-update) | async-done | bytes 524304 | tf_op jit(solution)/shard_map/reduce_scatter | solution.py:163
  (113 shorter events, 60.6 us)
Async XLA Ops:
  12.6 95.5 %all-to-all-start = ((s32[8,32,2]{1,2,0:T(2,128)}), s32[8,32,2]{1,2,0:T(2,128)S(1)}, u32[]{:S(2)}, u32[]{:S(2)}) async-start(s32[8,32,2]{1,2,0:T(2,128)} %pad_add_fusion), calls=%async_computation | async-start | bytes 16384 | tf_op jit(solution)/shard_map/all_to_all | solution.py:144
  19.9 84.7 %copy-start = (s32[16]{0:T(128)S(1)}, s32[16]{0:T(128)}, u32[]{:S(2)}) copy-start(s32[16]{0:T(128)} %param.11) | copy-start | bytes 196
  108.0 65.9 %all-to-all-start.1 = ((f32[8,32,2048]{2,1,0:T(8,128)}), f32[8,32,2048]{2,1,0:T(8,128)}, u32[]{:S(2)}, u32[]{:S(2)}) async-start(f32[8,32,2048]{2,1,0:T(8,128)} %bitcast.8), calls=%async_computation.1 | async-start | bytes 4194304 | tf_op jit(solution)/shard_map/all_to_all | solution.py:143
  114.0 197.2 %reduce-scatter.2.cloned.1.call-start = ((), (), s32[]{:S(2)}) async-start(), calls=%async_computation.4 | async-start | bytes 2621440 | tf_op jit(solution)/shard_map/reduce_scatter | solution.py:163
  115.0 19.5 %collective-permute-start = (f32[16,2048]{1,0:T(8,128)S(1)}, f32[16,2048]{1,0:T(8,128)S(1)}, u32[]{:S(2)}, u32[]{:S(2)}) collective-permute-start(f32[16,2048]{1,0:T(8,128)S(1)} %select_select_fusion), channel_id=1, source_target_pairs={{0,4},{4,0},{8,12},{12,8},{16,20},{20,16},{24,28},{28,24},{1,5},{5... | collective-permute-start | bytes 393224 | tf_op jit(solution)/shard_map/ppermute | solution.py:15
  134.5 16.2 %collective-permute-start.1 = (f32[16,2048]{1,0:T(8,128)S(1)}, f32[16,2048]{1,0:T(8,128)S(1)}, u32[]{:S(2)}, u32[]{:S(2)}) collective-permute-start(f32[16,2048]{1,0:T(8,128)S(1)} %fusion.42), channel_id=1, source_target_pairs={{0,8},{4,12},{8,0},{12,4},{16,24},{20,28},{24,16},{28,20},{1,9},{5... | collective-permute-start | bytes 393224 | tf_op jit(solution)/shard_map/ppermute | solution.py:15
  150.7 16.6 %collective-permute-start.2 = (f32[16,2048]{1,0:T(8,128)S(1)}, f32[16,2048]{1,0:T(8,128)S(1)}, u32[]{:S(2)}, u32[]{:S(2)}) collective-permute-start(f32[16,2048]{1,0:T(8,128)S(1)} %add.251), channel_id=1, source_target_pairs={{0,16},{4,20},{8,24},{12,28},{16,0},{20,4},{24,8},{28,12},{1,17},{... | collective-permute-start | bytes 393224 | tf_op jit(solution)/shard_map/ppermute | solution.py:15
  281.5 10.1 %all-to-all-start.2 = ((f32[8,1,32]{2,1,0:T(1,128)}), f32[8,1,32]{2,1,0:T(1,128)S(1)}, u32[]{:S(2)}, u32[]{:S(2)}) async-start(f32[8,1,32]{2,1,0:T(1,128)} %bitcast.11), calls=%async_computation.3 | async-start | bytes 8192 | tf_op jit(solution)/shard_map/all_to_all | solution.py:152
Sparse Core Ops, SparseCore 0:
  281.0 30.2 reduce-scatter.1
